TPU v7x, 32 devices: a whole 2x2x4 slice. The times are simulated.
32 devices in a mesh: fsdp: 8 (over y, x, core), rep: 4 (over z).
Axes of the slice: x: 2, y: 2, z: 4, core: 2. Of those that a mesh axis runs over, the one named last changes fastest.
Arguments:
- pseudo_grads: float32 [4, 96, 8192], P('rep', 'fsdp'), may hold values from -6 to 6
- counts: int32 [4], P('rep'), may hold values from 4000 to 10999, as said below
- master: float32 [96, 8192], P('fsdp'), may hold values from -6 to 6
- momentum: float32 [96, 8192], P('fsdp'), may hold values from -2 to 2
Outputs:
- new_fragment: bfloat16 [96, 8192], P('fsdp')
- new_master: float32 [96, 8192], P('fsdp')
- new_momentum: float32 [96, 8192], P('fsdp')
Inputs may be any that keep to these rules, and one draw needn't show every extreme that they name: kept-token counts of the replica groups, positive.
All inputs are finite; a program needn't handle non-finite values.
Results may differ from a plain program's by a relative error of at most 0.0004.
Values may be sent and summed in bfloat16 or wider, within the bound.
A program may use at most 64 MiB of HBM per device.

v0:
```python
import jax
import jax.numpy as jnp
from jax import lax
from jax.sharding import PartitionSpec as P

outer_momentum = 0.9
outer_rate = 0.7


def shards(pseudo_grads, counts, master, momentum):
    tokens_kept = counts.astype(jnp.float32)[0]
    weighted = tokens_kept * pseudo_grads[0]
    summed, all_tokens = lax.psum((weighted, tokens_kept), "rep")
    outer_grad = summed / all_tokens
    new_momentum = outer_momentum * momentum + outer_grad
    new_master = master - outer_rate * (outer_grad + outer_momentum * new_momentum)
    new_fragment = new_master.astype(jnp.bfloat16)
    return (new_fragment, new_master, new_momentum)


def solution(mesh):
    placed = (P("rep", "fsdp", None), P("rep"), P("fsdp", None), P("fsdp", None))
    return jax.shard_map(
        shards,
        mesh=mesh,
        in_specs=placed,
        out_specs=(P("fsdp", None), P("fsdp", None), P("fsdp", None)),
        check_vma=False,
    )
```

profile of v0, /device:TPU:0, one launch (start us, length us, event | category | flops | bytes accessed | tf_op | source)
XLA Modules:
  0.0 62.1 jit_solution(6913630390625272155)
XLA Ops:
  7.2 0.0 all-reduce.2.cloned.1.call-start
  7.9 0.0 copy-start
  7.9 0.0 copy-start.1
  7.9 2.1 %fusion = f32[12,8192]{1,0:T(8,128)} fusion(f32[1,12,8192]{2,0,1:T(1,128)} %param.4, f32[]{:T(128)} %bitcast), kind=kLoop, calls=%fused_computation.1 | loop fusion | flops 98304 | bytes 786436 | tf_op jit(solution)/shard_map/mul | solution.py:12
  10.0 0.0 all-reduce.2.cloned.1.call-update
  10.0 14.8 %psum.15 = f32[]{:T(128)} all-reduce(f32[]{:T(128)} %bitcast), channel_id=1, replica_groups=mesh['fsdp'=8,'rep'=4] {'rep'}, use_global_device_ids=true, to_apply=%region_1.0 | all-reduce | flops 1 | bytes 8 | tf_op jit(solution)/shard_map/psum | solution.py:13
  24.8 27.5 %all-reduce.2.cloned.1.call-done = f32[12,8192]{1,0:T(8,128)} async-done(((f32[12,8192]{1,0:T(8,128)}), f32[12,8192]{1,0:T(8,128)}) %all-reduce.2.cloned.1.call-update) | async-done | bytes 393232 | tf_op jit(solution)/shard_map/psum | solution.py:13
  52.3 0.0 copy-done
  52.3 0.0 copy-done.1
  52.3 2.9 %fusion.1 = (bf16[12,8192]{1,0:T(8,128)(2,1)}, f32[12,8192]{1,0:T(8,128)}, f32[12,8192]{1,0:T(8,128)}) fusion(f32[12,8192]{1,0:T(8,128)S(1)} %copy-done, f32[12,8192]{1,0:T(8,128)} %all-reduce.2.cloned.1.call-done, f32[]{:T(128)} %psum.15, f32[12,8192]{1,0:T(8,128)S(1)} %copy-done.1), kind=kLoop, calls=%fused_computation.5 | loop fusion | flops 786432 | bytes 2162692 | tf_op jit(solution)/shard_map/convert_element_type | solution.py:17
Async XLA Ops:
  7.2 45.1 %all-reduce.2.cloned.1.call-start = ((), (), s32[]{:S(2)}) async-start(), calls=%async_computation | async-start | bytes 1048576 | tf_op jit(solution)/shard_map/psum | solution.py:13
  7.9 44.4 %copy-start = (f32[12,8192]{1,0:T(8,128)S(1)}, f32[12,8192]{1,0:T(8,128)}, u32[]{:S(2)}) copy-start(f32[12,8192]{1,0:T(8,128)} %param.6) | copy-start | bytes 1179652
  7.9 44.4 %copy-start.1 = (f32[12,8192]{1,0:T(8,128)S(1)}, f32[12,8192]{1,0:T(8,128)}, u32[]{:S(2)}) copy-start(f32[12,8192]{1,0:T(8,128)} %param.7) | copy-start | bytes 1179652
Sparse Core Ops, SparseCore 0:
  10.9 41.3 all-reduce.1
where the time goes:
time: 62.3 us; the launch traced here: 62.1 us
  waiting for transfers between devices  27.5 us (44%)
  blocking collectives  14.8 us (24%)
  between operations  14.7 us (24%)
  other arithmetic  5.03 us (8%)
    psum x1, waiting for transfers between devices, shards(): summed, all_tokens = lax.psum((weighted, tokens_kept), 'rep')  27.5 us
    psum x1, blocking collectives, shards(): summed, all_tokens = lax.psum((weighted, tokens_kept), 'rep')  14.8 us
    convert_element_type x1, other arithmetic, shards(): new_fragment = new_master.astype(jnp.bfloat16)  2.91 us
    mul x1, other arithmetic, shards(): weighted = tokens_kept * pseudo_grads[0]  2.12 us
  transfers between devices with their start and end apart: 1, of which 1 were waited for; matrix products, arithmetic and copies ran while one was open for 0% of the time, Pallas kernels for 0%

commit v1 on v0

v1 whole, which is shorter than its diff:
```python
import functools

import jax
import jax.numpy as jnp
from jax import lax
from jax.experimental import pallas as pl
from jax.experimental.pallas import tpu as pltpu
from jax.sharding import PartitionSpec as P

outer_momentum = 0.9
outer_rate = 0.7

LANES = 128
CHUNKS = 8
LAG = 3
TOP = 32767.0
TINY = 1e-30
MESH = pl.DeviceIdType.MESH


def pieces(width):
    return [slice(k * LANES, (k + 1) * LANES) for k in range(width // LANES)]


def encode(parts):
    top = jnp.abs(parts[0])
    for part in parts[1:]:
        top = jnp.maximum(top, jnp.abs(part))
    top = jnp.maximum(jnp.max(top, axis=0, keepdims=True), TINY)
    inverse = TOP / top
    return [jnp.round(part * inverse) for part in parts], top * (1.0 / TOP)


def kernel(
    n, chunks, counts_ref, grads_ref, out_ref,
    own, inward, inward_meta, half, half_meta, total, total_meta,
    load_sem, send_a, send_b, recv_in, recv_half, recv_total,
):
    me = lax.axis_index("rep")
    middle = n // 2
    side = (me >= middle).astype(jnp.int32)
    step_in = 1 - 2 * side
    near, far = me + step_in, me - step_in
    is_middle = (me == middle - 1) | (me == middle)
    has_far = (me > 0) & (me < n - 1)
    width = own.shape[2]
    columns = pieces(width)

    def load(c):
        return pltpu.make_async_copy(
            grads_ref.at[0, :, pl.ds(c * width, width)], own.at[c], load_sem.at[c]
        )

    def remote(src, dst, send, recv, device):
        return pltpu.make_async_remote_copy(
            src_ref=src, dst_ref=dst, send_sem=send, recv_sem=recv,
            device_id={"rep": device}, device_id_type=MESH,
        )

    def to_near(c):
        return (
            remote(half.at[side, c], inward.at[c], send_a.at[c, 0], recv_in.at[c, 0], near),
            remote(half_meta.at[side, c], inward_meta.at[c], send_a.at[c, 1], recv_in.at[c, 1], near),
        )

    def across(c):
        return (
            remote(half.at[side, c], half.at[side, c], send_a.at[c, 0], recv_half.at[c, 0], near),
            remote(half_meta.at[side, c], half_meta.at[side, c], send_a.at[c, 1], recv_half.at[c, 1], near),
        )

    def arriving_half(c):
        return (
            remote(half.at[1 - side, c], half.at[1 - side, c], send_a.at[c, 0], recv_half.at[c, 0], near),
            remote(half_meta.at[1 - side, c], half_meta.at[1 - side, c], send_a.at[c, 1], recv_half.at[c, 1], near),
        )

    def to_far(c):
        return (
            remote(total.at[c], total.at[c], send_b.at[c, 0], recv_total.at[c, 0], far),
            remote(total_meta.at[c], total_meta.at[c], send_b.at[c, 1], recv_total.at[c, 1], far),
        )

    def start(copies):
        for copy in copies:
            copy.start()

    def wait_recv(copies):
        for copy in copies:
            copy.wait_recv()

    def wait_send(copies):
        for copy in copies:
            copy.wait_send()

    for c in range(chunks):
        load(c).start()

    barrier = pltpu.get_barrier_semaphore()

    @pl.when(me > 0)
    def _():
        pl.semaphore_signal(barrier, inc=1, device_id={"rep": me - 1}, device_id_type=MESH)

    @pl.when(me < n - 1)
    def _():
        pl.semaphore_signal(barrier, inc=1, device_id={"rep": me + 1}, device_id_type=MESH)

    tokens = jnp.full((1, LANES), counts_ref[0], jnp.int32).astype(jnp.float32)

    def keep_partial(c, parts, held):
        codes, step = encode(parts)
        for at, code in zip(columns, codes):
            half[side, c, :, at] = code.astype(jnp.int16)
        half_meta[side, c, 0:1, :] = step
        half_meta[side, c, 1:2, :] = held

    def own_partial(c):
        load(c).wait()
        keep_partial(c, [own[c, :, at] for at in columns], tokens)

    def joined_partial(c):
        load(c).wait()
        wait_recv(to_near(c))
        there = inward_meta[c, 1:2, :]
        held = there + tokens
        share, mine = there * inward_meta[c, 0:1, :] / held, tokens / held
        keep_partial(
            c,
            [inward[c, :, at].astype(jnp.float32) * share + own[c, :, at] * mine for at in columns],
            held,
        )

    def middle_total(c):
        wait_recv(arriving_half(c))
        low, high = half_meta[0, c, 1:2, :], half_meta[1, c, 1:2, :]
        all_tokens = low + high
        low_share = low * half_meta[0, c, 0:1, :] / all_tokens
        high_share = high * half_meta[1, c, 0:1, :] / all_tokens
        codes, step = encode(
            [
                half[0, c, :, at].astype(jnp.float32) * low_share
                + half[1, c, :, at].astype(jnp.float32) * high_share
                for at in columns
            ]
        )
        for at, code in zip(columns, codes):
            total[c, :, at] = code.astype(jnp.int16)
        total_meta[c, 0:1, :] = step

        @pl.when(has_far)
        def _():
            start(to_far(c))

        for k, code in enumerate(codes):
            out_ref[:, c * width + k * LANES : c * width + (k + 1) * LANES] = code * step

    def outer_total(c):
        wait_recv(to_far(c))

        @pl.when(has_far)
        def _():
            start(to_far(c))

        step = total_meta[c, 0:1, :]
        for k, at in enumerate(columns):
            out_ref[:, c * width + k * LANES : c * width + (k + 1) * LANES] = (
                total[c, :, at].astype(jnp.float32) * step
            )

    half_meta[side] = jnp.zeros(half_meta.shape[1:], jnp.float32)
    total_meta[...] = jnp.zeros(total_meta.shape, jnp.float32)

    pl.semaphore_wait(barrier, (me > 0).astype(jnp.int32) + (me < n - 1).astype(jnp.int32))

    if n > 3:
        @pl.when(is_middle)
        def _():
            for t in range(chunks + LAG):
                if t < chunks:
                    joined_partial(t)
                    start(across(t))
                if t >= LAG:
                    middle_total(t - LAG)

        @pl.when(jnp.logical_not(is_middle))
        def _():
            for c in range(chunks):
                @pl.when(has_far)
                def _():
                    joined_partial(c)

                @pl.when(jnp.logical_not(has_far))
                def _():
                    own_partial(c)

                start(to_near(c))
            for c in range(chunks):
                outer_total(c)
    else:
        for c in range(chunks):
            own_partial(c)
            start(across(c))
        for c in range(chunks):
            middle_total(c)

    for c in range(chunks):
        wait_send(to_near(c))

    @pl.when(has_far)
    def _():
        for c in range(chunks):
            wait_send(to_far(c))


def weighted_mean(n, counts, pseudo_grads):
    rows, depth = pseudo_grads.shape[1:]
    chunks = CHUNKS
    while depth % (chunks * LANES):
        chunks //= 2
    width = depth // chunks
    codes = functools.partial(pltpu.VMEM, dtype=jnp.int16)
    metas = functools.partial(pltpu.VMEM, dtype=jnp.float32)
    pairs = pltpu.SemaphoreType.DMA((chunks, 2))
    return pl.pallas_call(
        functools.partial(kernel, n, chunks),
        out_shape=jax.ShapeDtypeStruct((rows, depth), jnp.float32),
        in_specs=[
            pl.BlockSpec(memory_space=pltpu.SMEM),
            pl.BlockSpec(memory_space=pl.ANY),
        ],
        out_specs=pl.BlockSpec(memory_space=pltpu.VMEM),
        scratch_shapes=[
            pltpu.VMEM((chunks, rows, width), jnp.float32),
            codes((chunks, rows, width)),
            metas((chunks, 8, LANES)),
            codes((2, chunks, rows, width)),
            metas((2, chunks, 8, LANES)),
            codes((chunks, rows, width)),
            metas((chunks, 8, LANES)),
            pltpu.SemaphoreType.DMA((chunks,)),
            pairs, pairs, pairs, pairs, pairs,
        ],
        compiler_params=pltpu.CompilerParams(collective_id=0, has_side_effects=True),
    )(counts, pseudo_grads)


def solution(mesh):
    n = mesh.shape["rep"]

    def shards(pseudo_grads, counts, master, momentum):
        outer_grad = weighted_mean(n, counts, pseudo_grads) if n > 1 else pseudo_grads[0]
        new_momentum = outer_momentum * momentum + outer_grad
        new_master = master - outer_rate * (outer_grad + outer_momentum * new_momentum)
        new_fragment = new_master.astype(jnp.bfloat16)
        return (new_fragment, new_master, new_momentum)

    placed = (P("rep", "fsdp", None), P("rep"), P("fsdp", None), P("fsdp", None))
    return jax.shard_map(
        shards,
        mesh=mesh,
        in_specs=placed,
        out_specs=(P("fsdp", None), P("fsdp", None), P("fsdp", None)),
        check_vma=False,
    )
```

time: 62.3 us -> 25.6 us (0.41)
  waiting for transfers between devices: 27.5 us -> 0 us
  Pallas kernels: 0 us -> 19.8 us
  blocking collectives: 14.8 us -> 0 us
  between operations: 14.7 us -> 1.3 us
  other arithmetic: 5.03 us -> 2.22 us
  local copies, waits for them, and re-layouts: 0.01 us -> 2.04 us
    psum x1 -> x0, waiting for transfers between devices: 27.5 us -> none  [shards(): summed, all_tokens = lax.psum((weighted, tokens_kept), 'rep')]
    pallas_call x0 -> x1, Pallas kernels: none -> 19.8 us  [weighted_mean(): pl.pallas_call(functools.partial(kernel, n, chunks), out_shape=jax.ShapeD...]
    psum x1 -> x0, blocking collectives: 14.8 us -> none  [shards(): summed, all_tokens = lax.psum((weighted, tokens_kept), 'rep')]
    mul x1 -> x0, other arithmetic: 2.12 us -> none  [shards(): weighted = tokens_kept * pseudo_grads[0]]
    unnamed x4 -> x5, local copies, waits for them, and re-layouts: 0.01 us -> 2.04 us
    convert_element_type x1, other arithmetic: 2.91 us -> 2.22 us  [shards(): new_fragment = new_master.astype(jnp.bfloat16)]
  transfers between devices with their start and end apart: 1 -> 0, of which waited for: 1 -> 0; matrix products, arithmetic and copies ran while one was open for 0% -> 0% of each run, Pallas kernels for 0% -> 0%
where the time goes in v1:
time: 25.6 us; the launch traced here: 25.4 us
  Pallas kernels  19.8 us (77%)
  other arithmetic  2.22 us (9%)
  local copies, waits for them, and re-layouts  2.04 us (8%)
  between operations  1.3 us (5%)
    pallas_call x1, Pallas kernels, weighted_mean(): pl.pallas_call(functools.partial(kernel, n, chunks), out_shape=jax.ShapeD...  19.8 us
    convert_element_type x1, other arithmetic, shards(): new_fragment = new_master.astype(jnp.bfloat16)  2.22 us
    unnamed x5, local copies, waits for them, and re-layouts  2.04 us

profile of v1, /device:TPU:0, one launch (start us, length us, event | category | flops | bytes accessed | tf_op | source)
XLA Modules:
  0.0 25.4 jit_solution(9890861837604969581)
XLA Ops:
  1.3 2.0 %copy.7.grads_ref = f32[1,12,8192]{2,1,0:T(8,128)} copy(f32[1,12,8192]{2,0,1:T(1,128)} %param.4) | data formatting | bytes 786432 | tf_op args[0]
  3.3 0.0 copy-start
  3.3 0.0 copy-start.1
  3.3 19.8 %shard_map.67 = f32[12,8192]{1,0:T(8,128)} custom-call(s32[1]{0:T(128)S(6)} %copy.8.counts_ref, f32[1,12,8192]{2,1,0:T(8,128)} %copy.7.grads_ref), custom_call_target="tpu_custom_call" | custom-call | tf_op jit(solution)/shard_map/pallas_call | solution.py:225
  23.2 0.0 copy-done
  23.2 0.0 copy-done.1
  23.2 2.2 %fusion = (bf16[12,8192]{1,0:T(8,128)(2,1)}, f32[12,8192]{1,0:T(8,128)}, f32[12,8192]{1,0:T(8,128)}) fusion(f32[12,8192]{1,0:T(8,128)S(1)} %copy-done, f32[12,8192]{1,0:T(8,128)} %shard_map.67, f32[12,8192]{1,0:T(8,128)S(1)} %copy-done.1), kind=kLoop, calls=%fused_computation.2 | loop fusion | flops 688128 | bytes 2162688 | tf_op jit(solution)/shard_map/convert_element_type | solution.py:255
Async XLA Ops:
  3.3 19.8 %copy-start = (f32[12,8192]{1,0:T(8,128)S(1)}, f32[12,8192]{1,0:T(8,128)}, u32[]{:S(2)}) copy-start(f32[12,8192]{1,0:T(8,128)} %param.6) | copy-start | bytes 1179652
  3.3 19.9 %copy-start.1 = (f32[12,8192]{1,0:T(8,128)S(1)}, f32[12,8192]{1,0:T(8,128)}, u32[]{:S(2)}) copy-start(f32[12,8192]{1,0:T(8,128)} %param.7) | copy-start | bytes 1179652

commit v2 on v1

--- a/solution.py
+++ b/solution.py
@@ -11,15 +11,12 @@
 outer_rate = 0.7
 
 LANES = 128
-CHUNKS = 8
-LAG = 3
+SUBLANES = 8
+CHUNKS = 4
+LAG = 2
 TOP = 32767.0
 TINY = 1e-30
 MESH = pl.DeviceIdType.MESH
-
-
-def pieces(width):
-    return [slice(k * LANES, (k + 1) * LANES) for k in range(width // LANES)]
 
 
 def encode(parts):
@@ -43,12 +40,32 @@
     near, far = me + step_in, me - step_in
     is_middle = (me == middle - 1) | (me == middle)
     has_far = (me > 0) & (me < n - 1)
-    width = own.shape[2]
-    columns = pieces(width)
+    rows, tiles = own.shape[0], own.shape[1] // chunks
+    blocks = [(r, t) for r in range(rows) for t in range(0, tiles, SUBLANES)]
+
+    def put(ref, codes):
+        for k in range(0, len(codes), 2):
+            pair = jnp.concatenate(codes[k : k + 2], axis=0)
+            ref[k // 2, : pair.shape[0]] = pair.astype(jnp.int16)
+
+    def get(ref):
+        for k in range(0, len(blocks), 2):
+            pair = ref[k // 2].astype(jnp.float32)
+            yield pair[:SUBLANES]
+            if k + 1 < len(blocks):
+                yield pair[SUBLANES:]
+
+    def own_parts(c):
+        return [own[r, c * tiles + t : c * tiles + t + SUBLANES] for r, t in blocks]
+
+    def put_out(c, parts):
+        for (r, t), part in zip(blocks, parts):
+            at = c * tiles + t
+            out_ref[r // SUBLANES, at : at + SUBLANES, r % SUBLANES] = part
 
     def load(c):
         return pltpu.make_async_copy(
-            grads_ref.at[0, :, pl.ds(c * width, width)], own.at[c], load_sem.at[c]
+            grads_ref.at[:, pl.ds(c * tiles, tiles)], own.at[:, pl.ds(c * tiles, tiles)], load_sem.at[c]
         )
 
     def remote(src, dst, send, recv, device):
@@ -110,14 +127,13 @@
 
     def keep_partial(c, parts, held):
         codes, step = encode(parts)
-        for at, code in zip(columns, codes):
-            half[side, c, :, at] = code.astype(jnp.int16)
+        put(half.at[side, c], codes)
         half_meta[side, c, 0:1, :] = step
         half_meta[side, c, 1:2, :] = held
 
     def own_partial(c):
         load(c).wait()
-        keep_partial(c, [own[c, :, at] for at in columns], tokens)
+        keep_partial(c, own_parts(c), tokens)
 
     def joined_partial(c):
         load(c).wait()
@@ -127,7 +143,7 @@
         share, mine = there * inward_meta[c, 0:1, :] / held, tokens / held
         keep_partial(
             c,
-            [inward[c, :, at].astype(jnp.float32) * share + own[c, :, at] * mine for at in columns],
+            [there * share + here * mine for there, here in zip(get(inward.at[c]), own_parts(c))],
             held,
         )
 
@@ -139,21 +155,18 @@
         high_share = high * half_meta[1, c, 0:1, :] / all_tokens
         codes, step = encode(
             [
-                half[0, c, :, at].astype(jnp.float32) * low_share
-                + half[1, c, :, at].astype(jnp.float32) * high_share
-                for at in columns
+                low_part * low_share + high_part * high_share
+                for low_part, high_part in zip(get(half.at[0, c]), get(half.at[1, c]))
             ]
         )
-        for at, code in zip(columns, codes):
-            total[c, :, at] = code.astype(jnp.int16)
+        put(total.at[c], codes)
         total_meta[c, 0:1, :] = step
 
         @pl.when(has_far)
         def _():
             start(to_far(c))
 
-        for k, code in enumerate(codes):
-            out_ref[:, c * width + k * LANES : c * width + (k + 1) * LANES] = code * step
+        put_out(c, [code * step for code in codes])
 
     def outer_total(c):
         wait_recv(to_far(c))
@@ -163,10 +176,7 @@
             start(to_far(c))
 
         step = total_meta[c, 0:1, :]
-        for k, at in enumerate(columns):
-            out_ref[:, c * width + k * LANES : c * width + (k + 1) * LANES] = (
-                total[c, :, at].astype(jnp.float32) * step
-            )
+        put_out(c, [part * step for part in get(total.at[c])])
 
     half_meta[side] = jnp.zeros(half_meta.shape[1:], jnp.float32)
     total_meta[...] = jnp.zeros(total_meta.shape, jnp.float32)
@@ -215,34 +225,36 @@
 
 def weighted_mean(n, counts, pseudo_grads):
     rows, depth = pseudo_grads.shape[1:]
+    tiles = depth // LANES
     chunks = CHUNKS
-    while depth % (chunks * LANES):
+    while tiles % (chunks * SUBLANES):
         chunks //= 2
-    width = depth // chunks
-    codes = functools.partial(pltpu.VMEM, dtype=jnp.int16)
-    metas = functools.partial(pltpu.VMEM, dtype=jnp.float32)
+    code = (-(-(rows * tiles // SUBLANES // chunks) // 2), 2 * SUBLANES, LANES)
+    meta = (2, LANES)
+    groups = -(-rows // SUBLANES)
     pairs = pltpu.SemaphoreType.DMA((chunks, 2))
-    return pl.pallas_call(
+    out = pl.pallas_call(
         functools.partial(kernel, n, chunks),
-        out_shape=jax.ShapeDtypeStruct((rows, depth), jnp.float32),
+        out_shape=jax.ShapeDtypeStruct((groups, tiles, SUBLANES, LANES), jnp.float32),
         in_specs=[
             pl.BlockSpec(memory_space=pltpu.SMEM),
             pl.BlockSpec(memory_space=pl.ANY),
         ],
         out_specs=pl.BlockSpec(memory_space=pltpu.VMEM),
         scratch_shapes=[
-            pltpu.VMEM((chunks, rows, width), jnp.float32),
-            codes((chunks, rows, width)),
-            metas((chunks, 8, LANES)),
-            codes((2, chunks, rows, width)),
-            metas((2, chunks, 8, LANES)),
-            codes((chunks, rows, width)),
-            metas((chunks, 8, LANES)),
+            pltpu.VMEM((rows, tiles, LANES), jnp.float32),
+            pltpu.VMEM((chunks, *code), jnp.int16),
+            pltpu.VMEM((chunks, *meta), jnp.float32),
+            pltpu.VMEM((2, chunks, *code), jnp.int16),
+            pltpu.VMEM((2, chunks, *meta), jnp.float32),
+            pltpu.VMEM((chunks, *code), jnp.int16),
+            pltpu.VMEM((chunks, *meta), jnp.float32),
             pltpu.SemaphoreType.DMA((chunks,)),
             pairs, pairs, pairs, pairs, pairs,
         ],
         compiler_params=pltpu.CompilerParams(collective_id=0, has_side_effects=True),
-    )(counts, pseudo_grads)
+    )(counts, pseudo_grads.reshape(rows, tiles, LANES))
+    return out.transpose(0, 2, 1, 3).reshape(groups * SUBLANES, depth)[:rows]
 
 
 def solution(mesh):

time: 25.6 us -> 21.8 us (0.85)
  local copies, waits for them, and re-layouts: 2.04 us -> 0.01 us
  Pallas kernels: 19.8 us -> 17.9 us
    unnamed x5 -> x2, local copies, waits for them, and re-layouts: 2.04 us -> 0.01 us
    pallas_call x1, Pallas kernels: 19.8 us -> 17.9 us  [weighted_mean(): pl.pallas_call(functools.partial(kernel, n, chunks), out_shape=jax.ShapeD...]
where the time goes in v2:
time: 21.8 us; the launch traced here: 21.7 us
  Pallas kernels  17.9 us (82%)
  other arithmetic  2.38 us (11%)
  between operations  1.36 us (6%)
    pallas_call x1, Pallas kernels, weighted_mean(): pl.pallas_call(functools.partial(kernel, n, chunks), out_shape=jax.ShapeD...  17.9 us
    convert_element_type x1, other arithmetic, shards(): new_fragment = new_master.astype(jnp.bfloat16)  2.38 us

profile of v2, /device:TPU:0, one launch (start us, length us, event | category | flops | bytes accessed | tf_op | source)
XLA Modules:
  0.0 21.7 jit_solution(17034371400829306308)
XLA Ops:
  0.6 0.0 copy-start
  1.3 17.9 %shard_map.67 = f32[2,64,8,128]{3,2,1,0:T(8,128)} custom-call(s32[1]{0:T(128)S(6)} %copy.7.counts_ref, f32[12,64,128]{2,1,0:T(8,128)} %bitcast.5), custom_call_target="tpu_custom_call" | custom-call | tf_op jit(solution)/shard_map/pallas_call | solution.py:236
  19.3 0.0 copy-done
  19.3 2.4 %fusion = (bf16[12,8192]{1,0:T(8,128)(2,1)}, f32[12,8192]{1,0:T(8,128)}, f32[12,8192]{1,0:T(8,128)}) fusion(f32[12,8192]{1,0:T(8,128)S(1)} %copy-done, f32[16,8192]{1,0:T(8,128)} %bitcast.4, f32[12,8192]{1,0:T(8,128)} %param.7), kind=kLoop, calls=%fused_computation.2 | loop fusion | flops 688128 | bytes 2162688 | tf_op jit(solution)/shard_map/convert_element_type | solution.py:267
Async XLA Ops:
  0.6 18.7 %copy-start = (f32[12,8192]{1,0:T(8,128)S(1)}, f32[12,8192]{1,0:T(8,128)}, u32[]{:S(2)}) copy-start(f32[12,8192]{1,0:T(8,128)} %param.6) | copy-start | bytes 1179652

commit v3 on v2

--- a/solution.py
+++ b/solution.py
@@ -12,8 +12,9 @@
 
 LANES = 128
 SUBLANES = 8
-CHUNKS = 4
-LAG = 2
+CHUNKS = 8
+LAG = 5
+VLIM = 8 * 1024 * 1024
 TOP = 32767.0
 TINY = 1e-30
 MESH = pl.DeviceIdType.MESH
@@ -238,7 +239,7 @@
         out_shape=jax.ShapeDtypeStruct((groups, tiles, SUBLANES, LANES), jnp.float32),
         in_specs=[
             pl.BlockSpec(memory_space=pltpu.SMEM),
-            pl.BlockSpec(memory_space=pl.ANY),
+            pl.BlockSpec(memory_space=pltpu.HBM),
         ],
         out_specs=pl.BlockSpec(memory_space=pltpu.VMEM),
         scratch_shapes=[
@@ -252,8 +253,8 @@
             pltpu.SemaphoreType.DMA((chunks,)),
             pairs, pairs, pairs, pairs, pairs,
         ],
-        compiler_params=pltpu.CompilerParams(collective_id=0, has_side_effects=True),
-    )(counts, pseudo_grads.reshape(rows, tiles, LANES))
+        compiler_params=pltpu.CompilerParams(collective_id=0, has_side_effects=True, vmem_limit_bytes=VLIM),
+    )(counts, pltpu.with_memory_space_constraint(pseudo_grads.reshape(rows, tiles, LANES), pltpu.HBM))
     return out.transpose(0, 2, 1, 3).reshape(groups * SUBLANES, depth)[:rows]
 
 

time: 21.8 us -> 20.6 us (0.945)
  Pallas kernels: 17.9 us -> 16.8 us
    pallas_call x1, Pallas kernels: 17.9 us -> 16.8 us  [weighted_mean(): pl.pallas_call(functools.partial(kernel, n, chunks), out_shape=jax.ShapeD...]
where the time goes in v3:
time: 20.6 us; the launch traced here: 20.4 us
  Pallas kernels  16.8 us (82%)
  other arithmetic  2.22 us (11%)
  between operations  1.36 us (7%)
    pallas_call x1, Pallas kernels, weighted_mean(): pl.pallas_call(functools.partial(kernel, n, chunks), out_shape=jax.ShapeD...  16.8 us
    convert_element_type x1, other arithmetic, shards(): new_fragment = new_master.astype(jnp.bfloat16)  2.22 us

profile of v3, /device:TPU:0, one launch (start us, length us, event | category | flops | bytes accessed | tf_op | source)
XLA Modules:
  0.0 20.4 jit_solution(10422045006615639231)
XLA Ops:
  0.6 0.0 copy-start
  1.3 16.8 %shard_map.67 = f32[2,64,8,128]{3,2,1,0:T(8,128)S(1)} custom-call(s32[1]{0:T(128)S(6)} %copy.7.counts_ref, f32[12,64,128]{2,1,0:T(8,128)} %bitcast.5), custom_call_target="tpu_custom_call" | custom-call | tf_op jit(solution)/shard_map/pallas_call | solution.py:237
  18.2 0.0 copy-done
  18.2 2.2 %fusion = (bf16[12,8192]{1,0:T(8,128)(2,1)}, f32[12,8192]{1,0:T(8,128)}, f32[12,8192]{1,0:T(8,128)}) fusion(f32[12,8192]{1,0:T(8,128)S(1)} %copy-done, f32[16,8192]{1,0:T(8,128)S(1)} %bitcast.4, f32[12,8192]{1,0:T(8,128)} %param.7), kind=kLoop, calls=%fused_computation.2 | loop fusion | flops 688128 | bytes 2162688 | tf_op jit(solution)/shard_map/convert_element_type | solution.py:268
Async XLA Ops:
  0.6 17.5 %copy-start = (f32[12,8192]{1,0:T(8,128)S(1)}, f32[12,8192]{1,0:T(8,128)}, u32[]{:S(2)}) copy-start(f32[12,8192]{1,0:T(8,128)} %param.6) | copy-start | bytes 1179652

commit v4 on v3

--- a/solution.py
+++ b/solution.py
@@ -14,6 +14,7 @@
 SUBLANES = 8
 CHUNKS = 8
 LAG = 5
+PARTS = 4
 VLIM = 8 * 1024 * 1024
 TOP = 32767.0
 TINY = 1e-30
@@ -30,7 +31,7 @@
 
 
 def kernel(
-    n, chunks, counts_ref, grads_ref, out_ref,
+    n, chunks, counts_ref, grads_ref, momentum_ref, out_ref, momentum_out, momentum_sem,
     own, inward, inward_meta, half, half_meta, total, total_meta,
     load_sem, send_a, send_b, recv_in, recv_half, recv_total,
 ):
@@ -113,6 +114,8 @@
 
     for c in range(chunks):
         load(c).start()
+    momentum_load = pltpu.make_async_copy(momentum_ref, momentum_out, momentum_sem)
+    momentum_load.start()
 
     barrier = pltpu.get_barrier_semaphore()
 
@@ -215,6 +218,7 @@
         for c in range(chunks):
             middle_total(c)
 
+    momentum_load.wait()
     for c in range(chunks):
         wait_send(to_near(c))
 
@@ -224,7 +228,7 @@
             wait_send(to_far(c))
 
 
-def weighted_mean(n, counts, pseudo_grads):
+def weighted_mean(n, counts, pseudo_grads, momentum):
     rows, depth = pseudo_grads.shape[1:]
     tiles = depth // LANES
     chunks = CHUNKS
@@ -234,15 +238,20 @@
     meta = (2, LANES)
     groups = -(-rows // SUBLANES)
     pairs = pltpu.SemaphoreType.DMA((chunks, 2))
-    out = pl.pallas_call(
+    return pl.pallas_call(
         functools.partial(kernel, n, chunks),
-        out_shape=jax.ShapeDtypeStruct((groups, tiles, SUBLANES, LANES), jnp.float32),
+        out_shape=(
+            jax.ShapeDtypeStruct((groups, tiles, SUBLANES, LANES), jnp.float32),
+            jax.ShapeDtypeStruct((rows, depth), jnp.float32),
+        ),
         in_specs=[
             pl.BlockSpec(memory_space=pltpu.SMEM),
             pl.BlockSpec(memory_space=pltpu.HBM),
+            pl.BlockSpec(memory_space=pltpu.HBM),
         ],
-        out_specs=pl.BlockSpec(memory_space=pltpu.VMEM),
+        out_specs=(pl.BlockSpec(memory_space=pltpu.VMEM),) * 2,
         scratch_shapes=[
+            pltpu.SemaphoreType.DMA,
             pltpu.VMEM((rows, tiles, LANES), jnp.float32),
             pltpu.VMEM((chunks, *code), jnp.int16),
             pltpu.VMEM((chunks, *meta), jnp.float32),
@@ -254,19 +263,73 @@
             pairs, pairs, pairs, pairs, pairs,
         ],
         compiler_params=pltpu.CompilerParams(collective_id=0, has_side_effects=True, vmem_limit_bytes=VLIM),
-    )(counts, pltpu.with_memory_space_constraint(pseudo_grads.reshape(rows, tiles, LANES), pltpu.HBM))
-    return out.transpose(0, 2, 1, 3).reshape(groups * SUBLANES, depth)[:rows]
+    )(
+        counts,
+        pltpu.with_memory_space_constraint(pseudo_grads.reshape(rows, tiles, LANES), pltpu.HBM),
+        pltpu.with_memory_space_constraint(momentum, pltpu.HBM),
+    )
+
+
+def update_kernel(
+    grad_ref, master_ref, momentum_ref, fragment_ref, new_master_ref, new_momentum_ref,
+    fragment, new_master, new_momentum, sems,
+):
+    rows, depth = master_ref.shape
+    parts = sems.shape[1]
+    tiles = depth // LANES // parts
+    copies = []
+    for c in range(parts):
+        for low in range(0, rows, SUBLANES):
+            high = min(low + SUBLANES, rows)
+            for k in range(c * tiles, (c + 1) * tiles):
+                at = (slice(low, high), slice(k * LANES, (k + 1) * LANES))
+                outer_grad = grad_ref[low // SUBLANES, k, : high - low]
+                moved = outer_momentum * momentum_ref[at] + outer_grad
+                stepped = master_ref[at] - outer_rate * (outer_grad + outer_momentum * moved)
+                new_momentum[at] = moved
+                new_master[at] = stepped
+                fragment[at] = stepped.astype(jnp.bfloat16)
+        columns = pl.ds(c * tiles * LANES, tiles * LANES)
+        for k, (src, dst) in enumerate(
+            ((new_momentum, new_momentum_ref), (new_master, new_master_ref), (fragment, fragment_ref))
+        ):
+            copy = pltpu.make_async_copy(src.at[:, columns], dst.at[:, columns], sems.at[k, c])
+            copy.start()
+            copies.append(copy)
+    for copy in copies:
+        copy.wait()
+
+
+def update(outer_grad, master, momentum):
+    rows, depth = master.shape
+    parts = PARTS
+    while depth // LANES % parts:
+        parts //= 2
+    shapes = tuple(((rows, depth), kind) for kind in (jnp.bfloat16, jnp.float32, jnp.float32))
+    return pl.pallas_call(
+        update_kernel,
+        out_shape=tuple(jax.ShapeDtypeStruct(*shape) for shape in shapes),
+        in_specs=[pl.BlockSpec(memory_space=pltpu.VMEM)] * 3,
+        out_specs=(pl.BlockSpec(memory_space=pltpu.HBM),) * 3,
+        scratch_shapes=[
+            *(pltpu.VMEM(*shape) for shape in shapes),
+            pltpu.SemaphoreType.DMA((3, parts)),
+        ],
+        compiler_params=pltpu.CompilerParams(vmem_limit_bytes=VLIM),
+    )(outer_grad, master, momentum)
 
 
 def solution(mesh):
     n = mesh.shape["rep"]
 
     def shards(pseudo_grads, counts, master, momentum):
-        outer_grad = weighted_mean(n, counts, pseudo_grads) if n > 1 else pseudo_grads[0]
+        if n > 1:
+            outer_grad, momentum = weighted_mean(n, counts, pseudo_grads, momentum)
+            return update(outer_grad, master, momentum)
+        outer_grad = pseudo_grads[0]
         new_momentum = outer_momentum * momentum + outer_grad
         new_master = master - outer_rate * (outer_grad + outer_momentum * new_momentum)
-        new_fragment = new_master.astype(jnp.bfloat16)
-        return (new_fragment, new_master, new_momentum)
+        return (new_master.astype(jnp.bfloat16), new_master, new_momentum)
 
     placed = (P("rep", "fsdp", None), P("rep"), P("fsdp", None), P("fsdp", None))
     return jax.shard_map(

time: 20.6 us -> 19.5 us (0.947)
  other arithmetic: 2.22 us -> 0 us
  Pallas kernels: 16.8 us -> 18 us
    convert_element_type x1 -> x0, other arithmetic: 2.22 us -> none  [shards(): new_fragment = new_master.astype(jnp.bfloat16)]
    pallas_call x1 -> x2, Pallas kernels: 16.8 us -> 18 us  [the longest x1 16.8 us: weighted_mean(): pl.pallas_call(functools.partial(kernel, n, chunks), out_shape=(jax.Shape...]
where the time goes in v4:
time: 19.5 us; the launch traced here: 19.4 us
  Pallas kernels  18 us (92%)
  between operations  1.36 us (7%)
    pallas_call x1, Pallas kernels, weighted_mean(): pl.pallas_call(functools.partial(kernel, n, chunks), out_shape=(jax.Shape...  16.8 us
    pallas_call x1, Pallas kernels, update(): pl.pallas_call(update_kernel, out_shape=tuple((jax.ShapeDtypeStruct(*shap...  1.18 us

profile of v4, /device:TPU:0, one launch (start us, length us, event | category | flops | bytes accessed | tf_op | source)
XLA Modules:
  0.0 19.4 jit_solution(16096327213944229593)
XLA Ops:
  0.6 0.0 copy-start
  1.3 16.8 %shard_map.67 = (f32[2,64,8,128]{3,2,1,0:T(8,128)S(1)}, f32[12,8192]{1,0:T(8,128)S(1)}) custom-call(s32[1]{0:T(128)S(6)} %copy.7.counts_ref, f32[12,64,128]{2,1,0:T(8,128)} %bitcast.1, f32[12,8192]{1,0:T(8,128)} %momentum_ref.1), custom_call_target="tpu_custom_call" | custom-call | tf_op jit(solution)/shard_map/pallas_call | solution.py:241
  18.2 0.0 copy-done
  18.2 1.2 %shard_map.68 = (bf16[12,8192]{1,0:T(8,128)(2,1)}, f32[12,8192]{1,0:T(8,128)}, f32[12,8192]{1,0:T(8,128)}) custom-call(f32[2,64,8,128]{3,2,1,0:T(8,128)S(1)} %get-tuple-element.5.grad_ref, f32[12,8192]{1,0:T(8,128)S(1)} %copy-done, f32[12,8192]{1,0:T(8,128)S(1)} %get-tuple-element.6.momentum_ref), custom_call_target="tpu_custom_call" | custom-call | tf_op jit(solution)/shard_map/pallas_call | solution.py:309
Async XLA Ops:
  0.6 17.6 %copy-start = (f32[12,8192]{1,0:T(8,128)S(1)}, f32[12,8192]{1,0:T(8,128)}, u32[]{:S(2)}) copy-start(f32[12,8192]{1,0:T(8,128)} %master_ref.1) | copy-start | bytes 1179652
